TPU v7x, 32 devices: a whole 2x2x4 slice. The times are simulated.
32 devices in a mesh: seq: 8 (over z, x), chan: 4 (over y, core).
Axes of the slice: x: 2, y: 2, z: 4, core: 2. Of those that a mesh axis runs over, the one named last changes fastest.
Arguments:
- query: bfloat16 [2048, 4096], P('seq', 'chan'), may hold values from -6 to 6
- key_gate: bfloat16 [2048, 4096], P('seq', 'chan'), may hold values from -6 to 6
- value: bfloat16 [2048, 4096], P('seq', 'chan'), may hold values from -6 to 6
- group_order: int32 [16], replicated, may hold values from 0 to 15, each once
- emb_weight: float32 [33, 64], replicated, may hold values from -32 to 32
- emb_bias: float32 [64], replicated, may hold values from -1 to 1
- mid_weight: float32 [64, 64], replicated, may hold values from -0.75 to 0.75
- mid_bias: float32 [64], replicated, may hold values from -1 to 1
- out_filter: float32 [64, 4096], P(None, 'chan'), may hold values from -0.75 to 0.75
- decay_rate: float32 [4096], P('chan'), may hold values from 0.00014648438 to 0.0014648438
- skip_gain: float32 [4096], P('chan'), may hold values from 0.5 to 1.5
- out_weight: bfloat16 [4096, 4096], P('chan'), may hold values from -0.125 to 0.125
Outputs:
- projected: float32 [4096, 2048], P('chan', 'seq')
Inputs may be any that keep to these rules, and one draw needn't show every extreme that they name: `group_order`: a permutation of the group numbers.
All inputs are finite; a program needn't handle non-finite values.
Results may differ from a plain program's by a relative error of at most 0.011.
Values may be sent and summed in bfloat16 or wider, within the bound.
No kernel may reach another device: no remote copies, remote signals or barrier semaphores. Data moves between devices by JAX's collectives and lax.ppermute only.
A program may use at most 128 MiB of HBM per device.

v0:
```python
import math
import jax
import jax.numpy as jnp
from jax import lax
from jax.sharding import PartitionSpec as P

BLOCK = 128
sine_freq = 2.0


def transform_tables(block):
    period = 2 * block
    row_index = jnp.arange(block, dtype=jnp.int32)
    freq_index = jnp.arange(block + 1, dtype=jnp.int32)
    scale = math.pi / block
    angle_head = (freq_index[:, None] * row_index[None, :] % period).astype(jnp.float32) * scale
    fwd_head = jnp.concatenate([jnp.cos(angle_head), -jnp.sin(angle_head)], 0).astype(jnp.bfloat16)
    angle_tail = (freq_index[:, None] * (row_index[None, :] + block) % period).astype(
        jnp.float32
    ) * scale
    keep_cols = (row_index > 0).astype(jnp.float32)[None, :]
    fwd_tail = (jnp.concatenate([jnp.cos(angle_tail), -jnp.sin(angle_tail)], 0) * keep_cols).astype(
        jnp.bfloat16
    )
    weights = (
        jnp.where((freq_index == 0) | (freq_index == block), 1.0, 2.0).astype(jnp.float32) / period
    )
    angle_back = (row_index[:, None] * freq_index[None, :] % period).astype(jnp.float32) * scale
    inverse = jnp.concatenate(
        [jnp.cos(angle_back) * weights[None, :], -jnp.sin(angle_back) * weights[None, :]], 1
    ).astype(jnp.bfloat16)
    return (fwd_head, fwd_tail, inverse)


def filter_rows(
    positions, length, emb_weight, emb_bias, mid_weight, mid_bias, out_filter, decay_rate
):
    high = lax.Precision.HIGHEST
    time_float = positions.astype(jnp.float32)
    band_count = (emb_weight.shape[0] - 1) // 2
    band_index = jnp.arange(1, band_count + 1, dtype=jnp.int32)
    angles = (positions[:, None] * band_index[None, :] % length).astype(jnp.float32) * (
        2.0 * math.pi / length
    )
    embedded = jnp.concatenate([time_float[:, None] / length, jnp.cos(angles), jnp.sin(angles)], 1)
    hidden = jnp.sin(
        sine_freq * (jnp.dot(embedded, emb_weight, precision=high) + emb_bias[None, :])
    )
    hidden = jnp.sin(sine_freq * (jnp.dot(hidden, mid_weight, precision=high) + mid_bias[None, :]))
    filter_raw = jnp.dot(hidden, out_filter, precision=high)
    norm_scale = jnp.sqrt(-jnp.expm1(-2.0 * decay_rate))
    decayed = jnp.exp(-decay_rate[None, :] * time_float[:, None])
    return (filter_raw * decayed * norm_scale[None, :]).astype(jnp.bfloat16)


def local(
    query,
    key_gate,
    value,
    group_order,
    emb_weight,
    emb_bias,
    mid_weight,
    mid_bias,
    out_filter,
    decay_rate,
    skip_gain,
    out_weight,
):
    tok_rows, chan_width = query.shape
    my_groups = tok_rows // BLOCK
    seq_count = lax.axis_size("seq")
    length = tok_rows * seq_count
    total_groups = length // BLOCK
    half_rows = BLOCK + 1
    fwd_head, fwd_tail, inverse = transform_tables(BLOCK)
    seq_index = lax.axis_index("seq")
    mine = lax.dynamic_slice_in_dim(group_order, seq_index * my_groups, my_groups)
    signal = (key_gate.astype(jnp.float32) * value.astype(jnp.float32)).astype(jnp.bfloat16)
    positions = seq_index * tok_rows + jnp.arange(tok_rows, dtype=jnp.int32)
    own_rows = filter_rows(
        positions, length, emb_weight, emb_bias, mid_weight, mid_bias, out_filter, decay_rate
    )
    whole_filter = lax.all_gather(own_rows, "seq", axis=0, tiled=True)
    blocks = whole_filter.reshape(total_groups, BLOCK, chan_width)
    previous = jnp.concatenate([jnp.zeros((1, BLOCK, chan_width), jnp.bfloat16), blocks[:-1]], 0)

    def block_spectrum(blocks_pair):
        head_part = jnp.dot(fwd_head, blocks_pair[0], preferred_element_type=jnp.float32)
        tail_part = jnp.dot(fwd_tail, blocks_pair[1], preferred_element_type=jnp.float32)
        return (head_part + tail_part).astype(jnp.bfloat16)

    filter_spectrum = lax.map(block_spectrum, (blocks, previous))

    def accumulate(spectra_sum, spectrum, global_id):
        lag_index = mine - global_id
        causal = (lag_index >= 0).astype(jnp.float32)[:, None, None]
        picked = filter_spectrum[jnp.maximum(lag_index, 0)]
        filt_real = picked[:, :half_rows].astype(jnp.float32)
        filt_imag = picked[:, half_rows:].astype(jnp.float32)
        sig_real = spectrum[None, :half_rows].astype(jnp.float32)
        sig_imag = spectrum[None, half_rows:].astype(jnp.float32)
        real_part = filt_real * sig_real - filt_imag * sig_imag
        imag_part = filt_real * sig_imag + filt_imag * sig_real
        return spectra_sum + causal * jnp.concatenate([real_part, imag_part], 1)

    empty = jnp.zeros((my_groups, 2 * half_rows, chan_width), jnp.float32)

    def advance(running, element):
        spectrum = jnp.dot(fwd_head, element[0], preferred_element_type=jnp.float32).astype(
            jnp.bfloat16
        )
        return (accumulate(running, spectrum, element[1]), None)

    running, _ = lax.scan(
        advance,
        empty,
        (
            lax.all_gather(signal.reshape(my_groups, BLOCK, chan_width), "seq", axis=0, tiled=True),
            group_order,
        ),
    )
    out_spectrum = running.astype(jnp.bfloat16)
    convolved = jnp.einsum(
        "rk,nkc->nrc", inverse, out_spectrum, preferred_element_type=jnp.float32
    ).reshape(tok_rows, chan_width)
    mixed = (
        query.astype(jnp.float32) * (convolved + skip_gain[None, :] * signal.astype(jnp.float32))
    ).astype(jnp.bfloat16)
    return lax.psum_scatter(
        lax.dot_general(
            out_weight, mixed, (((0,), (1,)), ((), ())), preferred_element_type=jnp.float32
        ).astype(jnp.bfloat16),
        "chan",
        scatter_dimension=0,
        tiled=True,
    ).astype(jnp.float32)


def solution(mesh):
    return jax.shard_map(
        local,
        mesh=mesh,
        in_specs=(
            P("seq", "chan"),
            P("seq", "chan"),
            P("seq", "chan"),
            P(),
            P(),
            P(),
            P(),
            P(),
            P(None, "chan"),
            P("chan"),
            P("chan"),
            P("chan", None),
        ),
        out_specs=P("chan", "seq"),
        check_vma=False,
    )
```

profile of v0, /device:TPU:0, one launch (start us, length us, event | category | flops | bytes accessed | tf_op | source)
XLA Modules:
  0.0 414.4 jit_solution(10690862169828464235)
XLA Ops:
  7.5 1.5 fusion.23
  9.1 1.4 fusion.21
  10.5 1.9 fusion.19
  14.6 74.0 %all-gather.3.cloned.1.call-done = bf16[2048,1024]{1,0:T(8,128)(2,1)} async-done(((bf16[256,1024]{1,0:T(8,128)(2,1)}), bf16[2048,1024]{1,0:T(8,128)(2,1)}) %all-gather.3.cloned.1.call-update) | async-done | bytes 4194320 | tf_op jit(solution)/shard_map/all_gather | solution.py:84
  88.7 2.1 slice-done
  90.8 2.4 concatenate.22
  93.2 53.1 %while.21 = (s32[]{:T(128)}, bf16[16,258,1024]{2,1,0:T(8,128)(2,1)}, bf16[16,128,1024]{2,1,0:T(8,128)(2,1)}, bf16[258,128]{1,0:T(8,128)(2,1)S(1)}, bf16[16,128,1...) while((s32[]{:T(128)}, bf16[16,258,1024]{2,1,0:T(8,128)(2,1)}, ...), condition=%wide.region_1.2_spmd, body=%wide.region_0.1_spmd.sunk | while | flops 135794688 | bytes 3312205 | solution.py:93
  94.4 2.1 fusion.91
  97.8 2.1 fusion.91
  101.1 2.1 fusion.91
  104.4 2.1 fusion.91
  107.7 2.1 fusion.91
  111.0 2.0 fusion.91
  114.3 2.1 fusion.91
  117.6 2.1 fusion.91
  120.9 2.1 fusion.91
  124.3 2.1 fusion.91
  127.6 2.1 fusion.91
  130.9 2.1 fusion.91
  134.2 2.1 fusion.91
  137.6 2.0 fusion.91
  140.8 2.1 fusion.91
  144.2 2.1 fusion.91
  146.3 16.2 %all-gather.5.cloned.1.call-done = bf16[16,128,1024]{2,1,0:T(8,128)(2,1)} async-done(((bf16[2,128,1024]{2,1,0:T(8,128)(2,1)}), bf16[16,128,1024]{2,1,0:T(8,128)(2,1)}) %all-gather.5.cloned.1.call-update) | async-done | bytes 4194320 | tf_op jit(solution)/shard_map/all_gather | solution.py:119
  162.5 203.8 %while.22 = (s32[]{:T(128)}, f32[2,258,1024]{2,1,0:T(8,128)}, s32[16]{0:T(128)S(1)}, s32[2]{0:T(128)S(1)}, bf16[16,258,1024]{2,1,0:T(8,128)(2,1)}, /*index=5*/bf...) while((s32[]{:T(128)}, f32[2,258,1024]{2,1,0:T(8,128)}, ...), condition=%wide.region_3.4_spmd.clone, body=%wide.region_2.3_spmd.clone.sunk | while | flops 72389640 | bytes 15127731 | solution.py:115
  163.7 4.1 gather_fusion
  171.2 3.3 fusion.96
  175.8 4.1 gather_fusion
  183.3 4.0 fusion.96
  188.6 4.1 gather_fusion
  196.1 4.0 fusion.96
  201.4 4.1 gather_fusion
  208.9 4.0 fusion.96
  214.1 4.1 gather_fusion
  221.7 4.0 fusion.96
  226.9 4.1 gather_fusion
  234.4 4.0 fusion.96
  239.7 4.1 gather_fusion
  245.2 1.4 fusion.95
  247.2 4.0 fusion.96
  252.5 4.1 gather_fusion
  260.0 4.0 fusion.96
  265.3 4.1 gather_fusion
  272.8 4.0 fusion.96
  278.0 4.1 gather_fusion
  285.6 4.0 fusion.96
  290.8 4.1 gather_fusion
  298.3 4.0 fusion.96
  303.6 4.1 gather_fusion
  311.1 4.0 fusion.96
  316.4 4.1 gather_fusion
  321.8 1.4 fusion.95
  323.9 4.0 fusion.96
  329.2 4.1 gather_fusion
  334.6 1.4 fusion.95
  336.7 4.0 fusion.96
  341.9 4.1 gather_fusion
  349.5 4.0 fusion.96
  354.7 4.1 gather_fusion
  362.2 4.0 fusion.96
  366.3 2.2 fusion.24
  368.7 7.1 %fusion.17 = bf16[4096,256]{0,1:T(8,128)(2,1)} fusion(bf16[256,1024]{1,0:T(8,128)(2,1)S(1)} %fusion.27, bf16[1024,4096]{1,0:T(8,128)(2,1)} %param.27), kind=kOutput, calls=%fused_computation.31 | convolution fusion | flops 2148532224 | bytes 11010048 | tf_op jit(solution)/shard_map/dot_general | solution.py:131
  375.8 29.8 %reduce-scatter.2.cloned.1.call-done = bf16[1024,256]{0,1:T(8,128)(2,1)} async-done(((bf16[4096,256]{0,1:T(8,128)(2,1)}), bf16[1024,256]{0,1:T(8,128)(2,1)}) %reduce-scatter.2.cloned.1.call-update) | async-done | bytes 524304 | tf_op jit(solution)/shard_map/reduce_scatter | solution.py:130
  405.7 2.2 copy.14
  (164 shorter events, 93.3 us)
Async XLA Ops:
  6.5 4.0 copy-start
  6.5 5.9 %copy-start.3 = (bf16[256,1024]{1,0:T(8,128)(2,1)S(1)}, bf16[256,1024]{1,0:T(8,128)(2,1)}, u32[]{:S(2)}) copy-start(bf16[256,1024]{1,0:T(8,128)(2,1)} %param.17) | copy-start | bytes 1572868
  6.5 5.9 %copy-start.2 = (bf16[256,1024]{1,0:T(8,128)(2,1)S(1)}, bf16[256,1024]{1,0:T(8,128)(2,1)}, u32[]{:S(2)}) copy-start(bf16[256,1024]{1,0:T(8,128)(2,1)} %param.18) | copy-start | bytes 1572868
  6.5 82.1 %all-gather.3.cloned.1.call-start = ((), (), s32[]{:S(2)}) async-start(), calls=%async_computation.1 | async-start | bytes 4718592 | tf_op jit(solution)/shard_map/all_gather | solution.py:84
  10.5 4.0 copy-start.6
  12.4 150.1 %all-gather.5.cloned.1.call-start = ((), (), s32[]{:S(2)}) async-start(), calls=%async_computation.2 | async-start | bytes 4718592 | tf_op jit(solution)/shard_map/all_gather | solution.py:119
  13.5 392.2 %reduce-scatter.2.cloned.1.call-start = ((), (), s32[]{:S(2)}) async-start(), calls=%async_computation.3 | async-start | bytes 2621440 | tf_op jit(solution)/shard_map/reduce_scatter | solution.py:130
  88.7 2.1 slice-start
  366.3 2.2 copy-start.1
  366.3 2.2 copy-start.4
  366.3 2.2 copy-start.5
Sparse Core Ops, SparseCore 0:
  12.5 76.0 all-gather.2
  90.8 71.6 all-gather.4
  375.9 29.6 reduce-scatter.1
where the time goes:
time: 417 us; the launch traced here: 414 us
  waiting for transfers between devices  120 us (29%)
  other arithmetic  112 us (27%)
  matrix products  87 us (21%)
  local copies, waits for them, and re-layouts  81.3 us (19%)
  between operations  13.3 us (3%)
    all_gather x1, waiting for transfers between devices, local(): whole_filter = lax.all_gather(own_rows, 'seq', axis=0, tiled=True)  74 us
    gather x16, local copies, waits for them, and re-layouts, accumulate(): picked = filter_spectrum[jnp.maximum(lag_index, 0)]  65.2 us
    add x16, other arithmetic, accumulate(): return spectra_sum + causal * jnp.concatenate([real_part, imag_part], 1)  63.5 us
    dot_general x16, matrix products, block_spectrum(): jnp.dot(fwd_tail, blocks_pair[1], preferred_element_type=jnp.float32)  33.1 us
    reduce_scatter x1, waiting for transfers between devices, local(): lax.psum_scatter(lax.dot_general(out_weight, mixed, (((0,), (1,)), ((), (...  29.8 us
    sub x16, other arithmetic, accumulate(): real_part = filt_real * sig_real - filt_imag * sig_imag  22.4 us
    dot_general x16, matrix products, advance(): jnp.dot(fwd_head, element[0], preferred_element_type=jnp.float32)  19.9 us
    dot_general x16, matrix products, block_spectrum(): jnp.dot(fwd_head, blocks_pair[0], preferred_element_type=jnp.float32)  19.9 us
  transfers between devices with their start and end apart: 3, of which 3 were waited for; matrix products, arithmetic and copies ran while one was open for 14% of the time, Pallas kernels for 0%

commit v1 on v0

--- a/solution.py
+++ b/solution.py
@@ -6,6 +6,18 @@
 
 BLOCK = 128
 sine_freq = 2.0
+
+
+def _mix_windows(w_in, net_axis):
+    wide_n = lax.psum(1, net_axis)
+    by_place = [w_in]
+    for p in range(wide_n - 1):
+        by_place.append(
+            lax.ppermute(by_place[-1], net_axis, [(kk, (kk + 1) % wide_n) for kk in range(wide_n)])
+        )
+    return jnp.roll(
+        jnp.concatenate(by_place[::-1], 0), (lax.axis_index(net_axis) + 1) * w_in.shape[0], 0
+    )
 
 
 def transform_tables(block):
@@ -81,7 +93,7 @@
     own_rows = filter_rows(
         positions, length, emb_weight, emb_bias, mid_weight, mid_bias, out_filter, decay_rate
     )
-    whole_filter = lax.all_gather(own_rows, "seq", axis=0, tiled=True)
+    whole_filter = _mix_windows(own_rows, "seq")
     blocks = whole_filter.reshape(total_groups, BLOCK, chan_width)
     previous = jnp.concatenate([jnp.zeros((1, BLOCK, chan_width), jnp.bfloat16), blocks[:-1]], 0)
 

time: 417 us -> 440 us (1.055)
  waiting for transfers between devices: 120 us -> 136 us
    ppermute x0 -> x7, waiting for transfers between devices: none -> 108 us  [_mix_windows(): lax.ppermute(by_place[-1], net_axis, [(kk, (kk + 1) % wide_n) for kk in r...]
    all_gather x1 -> x0, waiting for transfers between devices: 74 us -> none  [local(): whole_filter = lax.all_gather(own_rows, 'seq', axis=0, tiled=True)]
    all_gather x1, waiting for transfers between devices: 16.2 us -> 0.01 us  [local(): lax.all_gather(signal.reshape(my_groups, BLOCK, chan_width), 'seq', axis=...]
  transfers between devices with their start and end apart: 3 -> 9, of which waited for: 3 -> 8; matrix products, arithmetic and copies ran while one was open for 14% -> 14% of each run, Pallas kernels for 0% -> 0%
where the time goes in v1:
time: 440 us; the launch traced here: 436 us
  waiting for transfers between devices  136 us (31%)
  other arithmetic  113 us (26%)
  matrix products  85.9 us (20%)
  local copies, waits for them, and re-layouts  83.3 us (19%)
  between operations  13.7 us (3%)
    ppermute x7, waiting for transfers between devices, _mix_windows(): lax.ppermute(by_place[-1], net_axis, [(kk, (kk + 1) % wide_n) for kk in r...  108 us
    gather x16, local copies, waits for them, and re-layouts, accumulate(): picked = filter_spectrum[jnp.maximum(lag_index, 0)]  65.2 us
    add x16, other arithmetic, accumulate(): return spectra_sum + causal * jnp.concatenate([real_part, imag_part], 1)  63.6 us
    dot_general x16, matrix products, block_spectrum(): jnp.dot(fwd_tail, blocks_pair[1], preferred_element_type=jnp.float32)  33 us
    reduce_scatter x1, waiting for transfers between devices, local(): lax.psum_scatter(lax.dot_general(out_weight, mixed, (((0,), (1,)), ((), (...  27.7 us
    sub x16, other arithmetic, accumulate(): real_part = filt_real * sig_real - filt_imag * sig_imag  22 us
    dot_general x16, matrix products, advance(): jnp.dot(fwd_head, element[0], preferred_element_type=jnp.float32)  19.9 us
    dot_general x16, matrix products, block_spectrum(): jnp.dot(fwd_head, blocks_pair[0], preferred_element_type=jnp.float32)  19.8 us
  transfers between devices with their start and end apart: 9, of which 8 were waited for; matrix products, arithmetic and copies ran while one was open for 14% of the time, Pallas kernels for 0%

profile of v1, /device:TPU:0, one launch (start us, length us, event | category | flops | bytes accessed | tf_op | source)
XLA Modules:
  0.0 436.5 jit_solution(3652854996209632523)
XLA Ops:
  11.5 3.0 collective-permute-start
  14.5 15.0 %collective-permute-done = bf16[256,1024]{1,0:T(8,128)(2,1)S(1)} collective-permute-done((bf16[256,1024]{1,0:T(8,128)(2,1)S(1)}, bf16[256,1024]{1,0:T(8,128)(2,1)S(1)}, u32[]{:S(2)}, u32[]{:S(2)}) %collective-permute-start) | collective-permute-done | bytes 524320 | tf_op jit(solution)/shard_map/ppermute | solution.py:16
  29.5 15.8 %collective-permute-done.1 = bf16[256,1024]{1,0:T(8,128)(2,1)S(1)} collective-permute-done((bf16[256,1024]{1,0:T(8,128)(2,1)S(1)}, bf16[256,1024]{1,0:T(8,128)(2,1)S(1)}, u32[]{:S(2)}, u32[]{:S(2)}) %collective-permute-start.1) | collective-permute-done | bytes 524320 | tf_op jit(solution)/shard_map/ppermute | solution.py:16
  45.3 14.9 %collective-permute-done.2 = bf16[256,1024]{1,0:T(8,128)(2,1)S(1)} collective-permute-done((bf16[256,1024]{1,0:T(8,128)(2,1)S(1)}, bf16[256,1024]{1,0:T(8,128)(2,1)S(1)}, u32[]{:S(2)}, u32[]{:S(2)}) %collective-permute-start.2) | collective-permute-done | bytes 524320 | tf_op jit(solution)/shard_map/ppermute | solution.py:16
  60.2 14.0 %collective-permute-done.3 = bf16[256,1024]{1,0:T(8,128)(2,1)S(1)} collective-permute-done((bf16[256,1024]{1,0:T(8,128)(2,1)S(1)}, bf16[256,1024]{1,0:T(8,128)(2,1)S(1)}, u32[]{:S(2)}, u32[]{:S(2)}) %collective-permute-start.3) | collective-permute-done | bytes 524320 | tf_op jit(solution)/shard_map/ppermute | solution.py:16
  74.1 2.2 multiply_convert_fusion
  77.2 10.0 %collective-permute-done.4 = bf16[256,1024]{1,0:T(8,128)(2,1)S(1)} collective-permute-done((bf16[256,1024]{1,0:T(8,128)(2,1)S(1)}, bf16[256,1024]{1,0:T(8,128)(2,1)S(1)}, u32[]{:S(2)}, u32[]{:S(2)}) %collective-permute-start.4) | collective-permute-done | bytes 524320 | tf_op jit(solution)/shard_map/ppermute | solution.py:16
  87.8 26.3 %collective-permute-done.5 = bf16[256,1024]{1,0:T(8,128)(2,1)S(1)} collective-permute-done((bf16[256,1024]{1,0:T(8,128)(2,1)S(1)}, bf16[256,1024]{1,0:T(8,128)(2,1)S(1)}, u32[]{:S(2)}, u32[]{:S(2)}) %collective-permute-start.5) | collective-permute-done | bytes 524320 | tf_op jit(solution)/shard_map/ppermute | solution.py:16
  115.1 12.5 %collective-permute-done.6 = bf16[256,1024]{1,0:T(8,128)(2,1)S(1)} collective-permute-done((bf16[256,1024]{1,0:T(8,128)(2,1)S(1)}, bf16[256,1024]{1,0:T(8,128)(2,1)S(1)}, u32[]{:S(2)}, u32[]{:S(2)}) %collective-permute-start.6) | collective-permute-done | bytes 524320 | tf_op jit(solution)/shard_map/ppermute | solution.py:16
  128.7 2.4 constant_dynamic-slice_fusion.1
  131.1 2.4 concatenate.29
  133.5 53.0 %while.21 = (s32[]{:T(128)}, bf16[16,258,1024]{2,1,0:T(8,128)(2,1)}, bf16[16,128,1024]{2,1,0:T(8,128)(2,1)}, bf16[258,128]{1,0:T(8,128)(2,1)S(1)}, bf16[16,128,1...) while((s32[]{:T(128)}, bf16[16,258,1024]{2,1,0:T(8,128)(2,1)}, ...), condition=%wide.region_1.2_spmd, body=%wide.region_0.1_spmd.sunk | while | flops 135794688 | bytes 3312205 | solution.py:105
  134.8 2.1 fusion.91
  138.1 2.1 fusion.91
  141.4 2.1 fusion.91
  144.7 2.0 fusion.91
  148.0 2.1 fusion.91
  151.3 2.0 fusion.91
  154.6 2.1 fusion.91
  157.9 2.0 fusion.91
  161.2 2.1 fusion.91
  164.5 2.1 fusion.91
  167.8 2.0 fusion.91
  171.1 2.1 fusion.91
  174.4 2.1 fusion.91
  181.0 2.1 fusion.91
  184.4 2.1 fusion.91
  186.5 202.6 %while.22 = (s32[]{:T(128)}, f32[2,258,1024]{2,1,0:T(8,128)}, s32[16]{0:T(128)S(1)}, s32[2]{0:T(128)S(1)}, bf16[16,258,1024]{2,1,0:T(8,128)(2,1)}, /*index=5*/bf...) while((s32[]{:T(128)}, f32[2,258,1024]{2,1,0:T(8,128)}, ...), condition=%wide.region_3.4_spmd.clone, body=%wide.region_2.3_spmd.clone.sunk | while | flops 72389640 | bytes 15127731 | solution.py:127
  187.8 4.1 gather_fusion
  195.2 3.3 fusion.96
  199.8 4.1 gather_fusion
  207.2 4.0 fusion.96
  212.5 4.1 gather_fusion
  219.9 4.0 fusion.96
  225.2 4.1 gather_fusion
  232.6 4.0 fusion.96
  237.9 4.1 gather_fusion
  245.3 4.0 fusion.96
  250.6 4.1 gather_fusion
  258.0 4.0 fusion.96
  263.3 4.1 gather_fusion
  270.8 4.0 fusion.96
  276.0 4.1 gather_fusion
  283.5 4.0 fusion.96
  288.7 4.1 gather_fusion
  296.2 4.0 fusion.96
  301.4 4.1 gather_fusion
  308.9 4.0 fusion.96
  314.1 4.1 gather_fusion
  321.6 4.0 fusion.96
  326.8 4.1 gather_fusion
  334.3 4.0 fusion.96
  339.5 4.1 gather_fusion
  347.0 4.0 fusion.96
  352.2 4.1 gather_fusion
  359.7 4.0 fusion.96
  365.0 4.1 gather_fusion
  372.4 4.0 fusion.96
  377.7 4.1 gather_fusion
  385.1 4.0 fusion.96
  389.1 2.1 fusion.24
  392.6 7.0 %fusion.17 = bf16[4096,256]{0,1:T(8,128)(2,1)} fusion(bf16[256,1024]{1,0:T(8,128)(2,1)S(1)} %fusion.27, bf16[1024,4096]{1,0:T(8,128)(2,1)} %param.27), kind=kOutput, calls=%fused_computation.31 | convolution fusion | flops 2148532224 | bytes 11010048 | tf_op jit(solution)/shard_map/dot_general | solution.py:143
  399.7 27.7 %reduce-scatter.2.cloned.1.call-done = bf16[1024,256]{0,1:T(8,128)(2,1)} async-done(((bf16[4096,256]{0,1:T(8,128)(2,1)}), bf16[1024,256]{0,1:T(8,128)(2,1)}) %reduce-scatter.2.cloned.1.call-update) | async-done | bytes 524304 | tf_op jit(solution)/shard_map/reduce_scatter | solution.py:142
  427.4 2.2 copy.14
  (189 shorter events, 104.6 us)
Async XLA Ops:
  6.5 3.9 copy-start
  6.5 179.9 %all-gather.2.cloned.1.call-start = ((), (), s32[]{:S(2)}) async-start(), calls=%async_computation.1 | async-start | bytes 4718592 | tf_op jit(solution)/shard_map/all_gather | solution.py:131
  11.5 18.0 %collective-permute-start = (bf16[256,1024]{1,0:T(8,128)(2,1)S(1)}, bf16[256,1024]{1,0:T(8,128)(2,1)S(1)}, u32[]{:S(2)}, u32[]{:S(2)}) collective-permute-start(bf16[256,1024]{1,0:T(8,128)(2,1)S(1)} %fusion.19), channel_id=1, source_target_pairs={{0,4},{4,8},{8,12},{12,16},{16,20},{20,24},{24,28},{28,0},{1,5},{5... | collective-permute-start | bytes 1572872 | tf_op jit(solution)/shard_map/ppermute | solution.py:16
  29.5 15.8 %collective-permute-start.1 = (bf16[256,1024]{1,0:T(8,128)(2,1)S(1)}, bf16[256,1024]{1,0:T(8,128)(2,1)S(1)}, u32[]{:S(2)}, u32[]{:S(2)}) collective-permute-start(bf16[256,1024]{1,0:T(8,128)(2,1)S(1)} %collective-permute-done), channel_id=1, source_target_pairs={{0,4},{4,8},{8,12},{12,16},{16,20},{20,24},{24,28},{28,0},{1,5},{5... | collective-permute-start | bytes 1572872 | tf_op jit(solution)/shard_map/ppermute | solution.py:16
  45.3 14.9 %collective-permute-start.2 = (bf16[256,1024]{1,0:T(8,128)(2,1)S(1)}, bf16[256,1024]{1,0:T(8,128)(2,1)S(1)}, u32[]{:S(2)}, u32[]{:S(2)}) collective-permute-start(bf16[256,1024]{1,0:T(8,128)(2,1)S(1)} %collective-permute-done.1), channel_id=1, source_target_pairs={{0,4},{4,8},{8,12},{12,16},{16,20},{20,24},{24,28},{28,0},{1,5},{5... | collective-permute-start | bytes 1572872 | tf_op jit(solution)/shard_map/ppermute | solution.py:16
  60.2 14.0 %collective-permute-start.3 = (bf16[256,1024]{1,0:T(8,128)(2,1)S(1)}, bf16[256,1024]{1,0:T(8,128)(2,1)S(1)}, u32[]{:S(2)}, u32[]{:S(2)}) collective-permute-start(bf16[256,1024]{1,0:T(8,128)(2,1)S(1)} %collective-permute-done.2), channel_id=1, source_target_pairs={{0,4},{4,8},{8,12},{12,16},{16,20},{20,24},{24,28},{28,0},{1,5},{5... | collective-permute-start | bytes 1572872 | tf_op jit(solution)/shard_map/ppermute | solution.py:16
  74.1 13.0 %collective-permute-start.4 = (bf16[256,1024]{1,0:T(8,128)(2,1)S(1)}, bf16[256,1024]{1,0:T(8,128)(2,1)S(1)}, u32[]{:S(2)}, u32[]{:S(2)}) collective-permute-start(bf16[256,1024]{1,0:T(8,128)(2,1)S(1)} %collective-permute-done.3), channel_id=1, source_target_pairs={{0,4},{4,8},{8,12},{12,16},{16,20},{20,24},{24,28},{28,0},{1,5},{5... | collective-permute-start | bytes 1572872 | tf_op jit(solution)/shard_map/ppermute | solution.py:16
  76.3 351.1 %reduce-scatter.2.cloned.1.call-start = ((), (), s32[]{:S(2)}) async-start(), calls=%async_computation.2 | async-start | bytes 2621440 | tf_op jit(solution)/shard_map/reduce_scatter | solution.py:142
  87.2 26.9 %collective-permute-start.5 = (bf16[256,1024]{1,0:T(8,128)(2,1)S(1)}, bf16[256,1024]{1,0:T(8,128)(2,1)S(1)}, u32[]{:S(2)}, u32[]{:S(2)}) collective-permute-start(bf16[256,1024]{1,0:T(8,128)(2,1)S(1)} %collective-permute-done.4), channel_id=1, source_target_pairs={{0,4},{4,8},{8,12},{12,16},{16,20},{20,24},{24,28},{28,0},{1,5},{5... | collective-permute-start | bytes 1572872 | tf_op jit(solution)/shard_map/ppermute | solution.py:16
  114.1 13.5 %collective-permute-start.6 = (bf16[256,1024]{1,0:T(8,128)(2,1)S(1)}, bf16[256,1024]{1,0:T(8,128)(2,1)S(1)}, u32[]{:S(2)}, u32[]{:S(2)}) collective-permute-start(bf16[256,1024]{1,0:T(8,128)(2,1)S(1)} %collective-permute-done.5), channel_id=1, source_target_pairs={{0,4},{4,8},{8,12},{12,16},{16,20},{20,24},{24,28},{28,0},{1,5},{5... | collective-permute-start | bytes 1572872 | tf_op jit(solution)/shard_map/ppermute | solution.py:16
  133.5 53.0 %copy-start.5 = (s32[16]{0:T(128)S(1)}, s32[16]{0:T(128)}, u32[]{:S(2)}) copy-start(s32[16]{0:T(128)} %param.19) | copy-start | bytes 196
  186.5 202.7 %copy-start.2 = (bf16[128,129]{0,1:T(8,128)(2,1)S(1)}, bf16[128,129]{0,1:T(8,128)(2,1)}, u32[]{:S(2)}) copy-start(bf16[128,129]{0,1:T(8,128)(2,1)} %get-tuple-element.134) | copy-start | bytes 99076
  186.5 202.7 %copy-start.3 = (bf16[128,129]{0,1:T(8,128)(2,1)S(1)}, bf16[128,129]{0,1:T(8,128)(2,1)}, u32[]{:S(2)}) copy-start(bf16[128,129]{0,1:T(8,128)(2,1)} %get-tuple-element.135) | copy-start | bytes 99076
  186.5 204.8 %copy-start.1 = (bf16[256,1024]{1,0:T(8,128)(2,1)S(1)}, bf16[256,1024]{1,0:T(8,128)(2,1)}, u32[]{:S(2)}) copy-start(bf16[256,1024]{1,0:T(8,128)(2,1)} %multiply_convert_fusion) | copy-start | bytes 1572868
  186.5 204.8 %copy-start.4 = (f32[1024]{0:T(1024)S(1)}, f32[1024]{0:T(1024)}, u32[]{:S(2)}) copy-start(f32[1024]{0:T(1024)} %param.26) | copy-start | bytes 12292
Sparse Core Ops, SparseCore 0:
  76.5 86.9 all-gather.1
  399.8 27.5 reduce-scatter.1
